TPU v7x, 32 devices: a whole 2x2x4 slice. The times are simulated.
32 devices in a mesh: section: 4 (over y, x), tile: 8 (over z, core).
Axes of the slice: x: 2, y: 2, z: 4, core: 2. Of those that a mesh axis runs over, the one named last changes fastest.
Arguments:
- stored_inputs: bfloat16 [4, 4, 24, 128, 1024], P('section', None, 'tile'), may hold values from -6 to 6
- cotangent: bfloat16 [4, 24, 128, 1024], P(None, 'tile'), may hold values from -6 to 6
- w_reduce: bfloat16 [4, 1024, 256], P('section'), may hold values from -0.1875 to 0.1875
- w_spatial: bfloat16 [4, 2304, 256], P('section'), may hold values from -0.125 to 0.125
- w_expand: bfloat16 [4, 256, 1024], P('section'), may hold values from -0.375 to 0.375
- bias_reduce: float32 [4, 256], P('section'), may hold values from -1 to 1
- bias_spatial: float32 [4, 256], P('section'), may hold values from -1 to 1
- bias_expand: float32 [4, 1024], P('section'), may hold values from 0.5 to 2
Outputs:
- input_grads: bfloat16 [4, 4, 24, 128, 1024], P('section', None, 'tile')
- grad_reduce: float32 [4, 1024, 256], P('section', 'tile')
- grad_spatial: float32 [4, 2304, 256], P('section', 'tile')
- grad_expand: float32 [4, 256, 1024], P('section', 'tile')
All inputs are finite; a program needn't handle non-finite values.
Results may differ from a plain program's by a relative error of at most 0.024.
Values may be sent and summed in bfloat16 or wider, within the bound.
A program may use at most 64 MiB of HBM per device.

v0:
```python
import functools

import jax
import jax.numpy as jnp
from jax import lax
from jax.experimental import pallas as pl
from jax.experimental.pallas import tpu as pltpu
from jax.sharding import PartitionSpec as P

BF = jnp.bfloat16
F32 = jnp.float32
PAD = 8
PIECES = 8
LAG = 2


def silu_and_slope(pre_act):
    sigma_val = jax.nn.sigmoid(pre_act)
    return pre_act * sigma_val, sigma_val * (1.0 + pre_act * (1.0 - sigma_val))


def dot_nn(left, right):
    return jnp.dot(left, right, preferred_element_type=F32)


def dot_tn(left, right):
    return lax.dot_general(left, right, (((0,), (0,)), ((), ())), preferred_element_type=F32)


def kernel(
    sections, tiles, x_ref, cot_ref, w1_ref, w2_ref, w3_ref, b1_ref, b2_ref, b3_ref,
    gin_ref, o1_ref, o2_ref, o3_ref,
    up, slope1, slope2, slope3, act_pad, taps, act2, g_pad, g3, g1,
    t1, t2, t3, fe_out, fe_in, be_out, be_in, sum1, sum2, sum3,
    p1, p2, p3, q1, q2, q3, r1, r2, r3, s1, s2, s3,
    cot_sem, up_ss, up_rs, fe_ss, fe_rs, be_ss, be_rs, a_ss, a_rs, z_ss, z_rs,
):
    micros, rows, cols, model = x_ref.shape
    bottle = w1_ref.shape[1]
    pixels = rows * cols
    width = cols // PIECES
    half = tiles // 2
    sec = lax.axis_index("section")
    tile = lax.axis_index("tile")
    core = lax.rem(tile, 2)
    zed = tile // 2
    is_last = sec == sections - 1
    has_above = tile > 0
    has_below = tile < tiles - 1
    partner = tile + 1 - 2 * core

    barrier = pltpu.get_barrier_semaphore()

    def greet(cond, target):
        @pl.when(cond)
        def _():
            pl.semaphore_signal(barrier, inc=1, device_id=target, device_id_type=pl.DeviceIdType.MESH)

    greet(has_above, {"tile": tile - 1})
    greet(has_below, {"tile": tile + 1})
    greet(sec > 0, {"section": sec - 1})
    greet(sec < sections - 1, {"section": sec + 1})
    for step in range(1, half):
        other = lax.rem(zed + step, half) * 2 + core
        pl.semaphore_signal(barrier, inc=1, device_id={"tile": other}, device_id_type=pl.DeviceIdType.MESH)

    def cot_copy(m):
        return pltpu.make_async_copy(cot_ref.at[m], up.at[m], cot_sem.at[m])

    @pl.when(is_last)
    def _():
        for m in range(micros):
            cot_copy(m).start()

    act_pad[...] = jnp.zeros(act_pad.shape, F32)
    g_pad[...] = jnp.zeros(g_pad.shape, F32)
    sum1[...] = jnp.zeros(sum1.shape, F32)
    sum2[...] = jnp.zeros(sum2.shape, F32)
    sum3[...] = jnp.zeros(sum3.shape, F32)

    def remote(src, dst, ss, rs, target):
        return pltpu.make_async_remote_copy(
            src_ref=src, dst_ref=dst, send_sem=ss, recv_sem=rs,
            device_id=target, device_id_type=pl.DeviceIdType.MESH,
        )

    def fe_up(m):
        return remote(fe_out.at[m, 0], fe_in.at[m, 1], fe_ss.at[m, 0], fe_rs.at[m, 1], {"tile": tile - 1})

    def fe_down(m):
        return remote(fe_out.at[m, 1], fe_in.at[m, 0], fe_ss.at[m, 1], fe_rs.at[m, 0], {"tile": tile + 1})

    def cut(j):
        return pl.ds(j * width, width)

    def be_up(m, j):
        n = m * PIECES + j
        return remote(
            be_out.at[m, 0, cut(j)], be_in.at[m, 1, cut(j)], be_ss.at[n, 0], be_rs.at[n, 1],
            {"tile": tile - 1},
        )

    def be_down(m, j):
        n = m * PIECES + j
        return remote(
            be_out.at[m, 1, cut(j)], be_in.at[m, 0, cut(j)], be_ss.at[n, 1], be_rs.at[n, 0],
            {"tile": tile + 1},
        )

    def relay(m, j):
        n = m * PIECES + j
        return remote(
            gin_ref.at[m, :, cut(j)], up.at[m, :, cut(j)], up_ss.at[n], up_rs.at[n],
            {"section": sec - 1},
        )

    def reduce_in(m, _):
        for y in range(rows):
            pre = dot_nn(x_ref[m, y], w1_ref[...]) + b1_ref[...]
            act, slope = silu_and_slope(pre)
            slope1[m, y] = slope
            act = act.astype(BF)
            act_pad[m, y + 1, pl.ds(PAD, cols)] = act.astype(F32)
            if y == 0:
                fe_out[m, 0] = act
            if y == rows - 1:
                fe_out[m, 1] = act
        return 0

    reduce_in(0, 0)

    greetings = (
        has_above.astype(jnp.int32) + has_below.astype(jnp.int32) + (sec > 0).astype(jnp.int32)
        + (sec < sections - 1).astype(jnp.int32) + (half - 1)
    )
    pl.semaphore_wait(barrier, greetings)

    def share_rims(m):
        @pl.when(has_above)
        def _():
            fe_up(m).start()

        @pl.when(has_below)
        def _():
            fe_down(m).start()

    def reduce_and_share(m, _):
        reduce_in(m, 0)
        share_rims(m)
        return 0

    share_rims(0)
    for n in range(model // bottle):
        lanes = pl.ds(n * bottle, bottle)
        t1[:, lanes] = w1_ref[lanes, :].astype(F32).T.astype(BF)
        t3[lanes, :] = w3_ref[:, lanes].astype(F32).T.astype(BF)
    for n in range(9):
        band = pl.ds(n * bottle, bottle)
        t2[band, :] = w2_ref[band, :].astype(F32).T.astype(BF)
    lax.fori_loop(1, micros, reduce_and_share, 0)

    def expand_out(m, _):
        @pl.when(has_above)
        def _():
            fe_down(m).wait_recv()
            act_pad[m, 0, pl.ds(PAD, cols)] = fe_in[m, 0].astype(F32)

        @pl.when(has_below)
        def _():
            fe_up(m).wait_recv()
            act_pad[m, rows + 1, pl.ds(PAD, cols)] = fe_in[m, 1].astype(F32)

        for shift in range(3):
            for y in range(rows + 2):
                taps[shift, m, y] = act_pad[m, y, pl.ds(PAD - 1 + shift, cols)].astype(BF)
        for y in range(rows):
            patch = jnp.concatenate(
                [taps[dx, m, y + dy] for dy in range(3) for dx in range(3)], axis=-1
            )
            pre = dot_nn(patch, w2_ref[...]) + b2_ref[...]
            act, slope = silu_and_slope(pre)
            slope2[m, y] = slope
            act = act.astype(BF)
            act2[m, y] = act
            for n in range(model // bottle):
                lanes = pl.ds(n * bottle, bottle)
                pre = dot_nn(act, w3_ref[:, lanes]) + b3_ref[:, lanes] + x_ref[m, y, :, lanes].astype(F32)
                slope3[m, y, :, lanes] = silu_and_slope(pre)[1]
        return 0

    @pl.when(jnp.logical_not(is_last))
    def _():
        lax.fori_loop(0, micros, expand_out, 0)

    def outer_part(m, j):
        @pl.when(jnp.logical_not(is_last))
        def _():
            relay(m, j).wait_recv()

        for y in range(rows):
            g3[y, cut(j)] = (up[m, y, cut(j)].astype(F32) * slope3[m, y, cut(j)]).astype(BF)
        back = dot_nn(g3[:, cut(j)].reshape(rows * width, model), t3[...])
        g2 = (back.reshape(rows, width, bottle) * slope2[m, :, cut(j)]).astype(BF)
        g_pad[m, pl.ds(1, rows), pl.ds(PAD + j * width, width)] = g2.astype(F32)
        be_out[m, 0, cut(j)] = g2[0]
        be_out[m, 1, cut(j)] = g2[rows - 1]

        @pl.when(has_above)
        def _():
            be_up(m, j).start()

        @pl.when(has_below)
        def _():
            be_down(m, j).start()

    def take_rims(m, j):
        @pl.when(has_above)
        def _():
            be_down(m, j).wait_recv()
            g_pad[m, 0, pl.ds(PAD + j * width, width)] = be_in[m, 0, cut(j)].astype(F32)

        @pl.when(has_below)
        def _():
            be_up(m, j).wait_recv()
            g_pad[m, rows + 1, pl.ds(PAD + j * width, width)] = be_in[m, 1, cut(j)].astype(F32)

    def inner_part(m, j):
        moved = [
            g_pad[m, :, pl.ds(PAD + 1 + j * width - dx, width)].astype(BF) for dx in range(3)
        ]
        patch = jnp.concatenate(
            [
                moved[dx][2 - dy : 2 - dy + rows].reshape(rows * width, bottle)
                for dy in range(3)
                for dx in range(3)
            ],
            axis=-1,
        )
        total = dot_nn(patch, t2[...])
        grad = (total.reshape(rows, width, bottle) * slope1[m, :, cut(j)]).astype(BF)
        g1[:, cut(j)] = grad
        flat = grad.reshape(rows * width, bottle)
        for n in range(model // bottle):
            lanes = pl.ds(n * bottle, bottle)
            back = dot_nn(flat, t1[:, lanes]).reshape(rows, width, bottle)
            direct = up[m, :, cut(j), lanes].astype(F32) * slope3[m, :, cut(j), lanes]
            gin_ref[m, :, cut(j), lanes] = (back + direct).astype(BF)

        @pl.when(sec > 0)
        def _():
            relay(m, j).start()

    def backward(m, _):
        @pl.when(is_last)
        def _():
            expand_out(m, 0)
            cot_copy(m).wait()

        for j in range(PIECES):
            outer_part(m, j)
            if j >= LAG:
                take_rims(m, j - LAG)
            if j > LAG:
                inner_part(m, j - LAG - 1)
        for j in range(PIECES - LAG, PIECES):
            take_rims(m, j)
            inner_part(m, j - 1)
        inner_part(m, PIECES - 1)
        sum3[...] += dot_tn(act2[m].reshape(pixels, bottle), g3[...].reshape(pixels, model))
        g2 = g_pad[m, pl.ds(1, rows), pl.ds(PAD, cols)].astype(BF).reshape(pixels, bottle)
        for dy in range(3):
            for dx in range(3):
                patch = taps[dx, m, pl.ds(dy, rows)].reshape(pixels, bottle)
                sum2[pl.ds((3 * dy + dx) * bottle, bottle)] += dot_tn(patch, g2)
        sum1[...] += dot_tn(x_ref[m].reshape(pixels, model), g1[...].reshape(pixels, bottle))
        return 0

    lax.fori_loop(0, micros, backward, 0)

    kinds = (
        (sum3, p3, q3, r3, s3, o3_ref),
        (sum2, p2, q2, r2, s2, o2_ref),
        (sum1, p1, q1, r1, s1, o1_ref),
    )

    def swap(kind):
        total, sent, got, _, _, _ = kinds[kind]
        return remote(sent, got, a_ss.at[kind], a_rs.at[kind], {"tile": partner})

    def spread(kind, step):
        _, _, _, part, landed, _ = kinds[kind]
        there = lax.rem(zed + step, half)
        n = kind * half + step
        return remote(
            part.at[there], landed.at[step - 1], z_ss.at[n], z_rs.at[n], {"tile": there * 2 + core}
        )

    for kind, (total, sent, _, _, _, out) in enumerate(kinds):
        span = out.shape[0]
        for z in range(half):
            first = pl.multiple_of((2 * z + 1 - core) * span, 16)
            sent[z] = total[pl.ds(first, span)].astype(BF)
        swap(kind).start()
    for kind, (total, _, got, part, _, out) in enumerate(kinds):
        span = out.shape[0]
        swap(kind).wait_recv()
        for z in range(half):
            first = pl.multiple_of((2 * z + core) * span, 16)
            part[z] = (total[pl.ds(first, span)] + got[z].astype(F32)).astype(BF)
        for step in range(1, half):
            spread(kind, step).start()
        own = pl.multiple_of((2 * zed + core) * span, 16)
        out[...] = total[pl.ds(own, span)] + got[zed].astype(F32)
    for kind, (_, _, _, _, landed, out) in enumerate(kinds):
        value = out[...]
        for step in range(1, half):
            spread(kind, step).wait_recv()
            value = value + landed[step - 1].astype(F32)
        out[...] = value

    def close(m, _):
        @pl.when(has_above)
        def _():
            fe_up(m).wait_send()
            for j in range(PIECES):
                be_up(m, j).wait_send()

        @pl.when(has_below)
        def _():
            fe_down(m).wait_send()
            for j in range(PIECES):
                be_down(m, j).wait_send()

        @pl.when(sec > 0)
        def _():
            for j in range(PIECES):
                relay(m, j).wait_send()

        return 0

    lax.fori_loop(0, micros, close, 0)
    for kind in range(3):
        swap(kind).wait_send()
        for step in range(1, half):
            spread(kind, step).wait_send()


def local(
    sections, tiles,
    stored_inputs, cotangent, w_reduce, w_spatial, w_expand, bias_reduce, bias_spatial, bias_expand,
):
    _, micros, rows, cols, model = stored_inputs.shape
    bottle = w_reduce.shape[2]
    half = tiles // 2
    spans = (model // tiles, 9 * bottle // tiles, bottle // tiles)
    wides = (bottle, bottle, model)
    vmem = pltpu.VMEM
    dma = pltpu.SemaphoreType.DMA
    whole = pl.BlockSpec(memory_space=pltpu.VMEM)
    scratch = [
        vmem((micros, rows, cols, model), BF),
        vmem((micros, rows, cols, bottle), F32),
        vmem((micros, rows, cols, bottle), F32),
        vmem((micros, rows, cols, model), F32),
        vmem((micros, rows + 2, cols + 2 * PAD, bottle), F32),
        vmem((3, micros, rows + 2, cols, bottle), BF),
        vmem((micros, rows, cols, bottle), BF),
        vmem((micros, rows + 2, cols + 2 * PAD, bottle), F32),
        vmem((rows, cols, model), BF),
        vmem((rows, cols, bottle), BF),
    ]
    scratch += [vmem((bottle, model), BF), vmem((9 * bottle, bottle), BF), vmem((model, bottle), BF)]
    scratch += [vmem((micros, 2, cols, bottle), BF)] * 4
    scratch += [vmem((span * tiles, wide), F32) for span, wide in zip(spans, wides)]
    for count in (half, half, half, half - 1):
        scratch += [vmem((count, span, wide), BF) for span, wide in zip(spans, wides)]
    pieces = micros * PIECES
    scratch += [
        dma((micros,)), dma((pieces,)), dma((pieces,)), dma((micros, 2)), dma((micros, 2)),
        dma((pieces, 2)), dma((pieces, 2)), dma((3,)), dma((3,)), dma((3 * half,)), dma((3 * half,)),
    ]
    outs = pl.pallas_call(
        functools.partial(kernel, sections, tiles),
        out_shape=[jax.ShapeDtypeStruct((micros, rows, cols, model), BF)]
        + [jax.ShapeDtypeStruct((span, wide), F32) for span, wide in zip(spans, wides)],
        in_specs=[whole, pl.BlockSpec(memory_space=pl.ANY)] + [whole] * 6,
        out_specs=[whole] * 4,
        scratch_shapes=scratch,
        compiler_params=pltpu.CompilerParams(
            collective_id=0, has_side_effects=True, vmem_limit_bytes=66 * 1024 * 1000
        ),
    )(
        stored_inputs[0], cotangent, w_reduce[0], w_spatial[0], w_expand[0],
        bias_reduce, bias_spatial, bias_expand,
    )
    return tuple(out[None] for out in outs)


def solution(mesh):
    return jax.shard_map(
        functools.partial(local, mesh.shape["section"], mesh.shape["tile"]),
        mesh=mesh,
        in_specs=(
            P("section", None, "tile", None, None),
            P(None, "tile", None, None),
            P("section", None, None),
            P("section", None, None),
            P("section", None, None),
            P("section", None),
            P("section", None),
            P("section", None),
        ),
        out_specs=(
            P("section", None, "tile", None, None),
            P("section", "tile", None),
            P("section", "tile", None),
            P("section", "tile", None),
        ),
        check_vma=False,
    )
```

profile of v0, /device:TPU:0, one launch (start us, length us, event | category | flops | bytes accessed | tf_op | source)
XLA Modules:
  0.0 149.4 jit_solution(3086620537660416161)
XLA Ops:
  0.6 142.8 %shard_map.111 = (bf16[4,3,128,1024]{3,2,1,0:T(8,128)(2,1)}, f32[128,256]{1,0:T(8,128)}, f32[288,256]{1,0:T(8,128)}, f32[32,1024]{1,0:T(8,128)}) custom-call(bf16[4,3,128,1024]{3,2,1,0:T(8,128)(2,1)} %bitcast.8, bf16[4,3,128,1024]{3,2,1,0:T(8,128)(2,1)} %cot_ref.1, bf16[1024,256]{1,0:T(8,128)(2,1)} %bitcast.11, bf16[2304,256]{1,0:T(8,128)(2,1)} %bitcast.10, ...), custom_call_target="tpu_custom_call" | custom-call | tf_op jit(solution)/shard_map/pallas_call | solution.py:382
  143.5 0.0 copy-start.2
  143.5 0.0 copy-start
  143.5 0.0 copy-start.1
  143.5 3.9 %copy.16 = bf16[1,4,3,128,1024]{4,3,2,1,0:T(8,128)(2,1)} copy(bf16[1,4,3,128,1024]{4,3,2,1,0:T(8,128)(2,1)} %bitcast.9) | data formatting | bytes 6291456
  147.4 0.0 copy-done.2
  147.4 0.7 copy.17
  148.1 0.0 copy-done
  148.1 0.7 copy.18
  148.8 0.0 copy-done.1
  148.8 0.7 copy.19
Async XLA Ops:
  143.5 3.9 %copy-start.2 = (f32[128,256]{1,0:T(8,128)S(1)}, f32[128,256]{1,0:T(8,128)}, u32[]{:S(2)}) copy-start(f32[128,256]{1,0:T(8,128)} %get-tuple-element.9) | copy-start | bytes 393220
  143.5 4.6 %copy-start = (f32[288,256]{1,0:T(8,128)S(1)}, f32[288,256]{1,0:T(8,128)}, u32[]{:S(2)}) copy-start(f32[288,256]{1,0:T(8,128)} %get-tuple-element.10) | copy-start | bytes 884740
  143.5 5.3 %copy-start.1 = (f32[32,1024]{1,0:T(8,128)S(1)}, f32[32,1024]{1,0:T(8,128)}, u32[]{:S(2)}) copy-start(f32[32,1024]{1,0:T(8,128)} %get-tuple-element.11) | copy-start | bytes 393220
where the time goes:
time: 150 us; the launch traced here: 149 us
  Pallas kernels  143 us (95%)
  local copies, waits for them, and re-layouts  5.95 us (4%)
    pallas_call x1, Pallas kernels, local(): pl.pallas_call(functools.partial(kernel, sections, tiles), out_shape=[jax...  143 us
    unnamed x10, local copies, waits for them, and re-layouts  5.95 us

commit v1 on v0

v1 whole, which is shorter than its diff:
```python
import functools

import jax
import jax.numpy as jnp
from jax import lax
from jax.experimental import pallas as pl
from jax.experimental.pallas import tpu as pltpu
from jax.sharding import PartitionSpec as P

BF = jnp.bfloat16
F32 = jnp.float32
PAD = 8
WIDTH = 16
TAPER = 8


def silu_and_slope(pre_act):
    sigma_val = jax.nn.sigmoid(pre_act)
    return pre_act * sigma_val, sigma_val * (1.0 + pre_act * (1.0 - sigma_val))


def dot_nn(left, right):
    return jnp.dot(left, right, preferred_element_type=F32)


def dot_tn(left, right):
    return lax.dot_general(left, right, (((0,), (0,)), ((), ())), preferred_element_type=F32)


def kernel(
    sections, tiles, x_in, cot_ref, w1_in, w2_in, w3_in, b1_ref, b2_ref, b3_ref,
    gin_out, o1_ref, o2_ref, o3_ref,
    x_ref, w1_ref, w2_ref, w3_ref, gin_ref,
    up, slope1, slope2, slope3, act_pad, taps, act2, g_pad, g3, g2, g1,
    t1, t2, t3, fe_out, fe_in, be_out, be_in, sum1, sum2, sum3,
    p1, p2, p3, q1, q2, q3, r1, r2, r3, u1, u2, u3, d1, d2, d3,
    x_sem, w_sem, gin_sem, cot_sem, up_ss, up_rs, fe_ss, fe_rs, be_ss, be_rs, a_ss, a_rs, z_ss, zu_rs, zd_rs,
):
    micros, rows, cols, model = x_ref.shape
    bottle = w1_ref.shape[1]
    pixels = rows * cols
    cuts = cut_columns(cols)
    pieces = len(cuts)
    half = tiles // 2
    sec = lax.axis_index("section")
    tile = lax.axis_index("tile")
    core = lax.rem(tile, 2)
    zed = tile // 2
    is_last = sec == sections - 1
    has_above = tile > 0
    has_below = tile < tiles - 1
    chip_above = zed > 0
    chip_below = zed < half - 1
    partner = tile + 1 - 2 * core

    def x_copy(m):
        return pltpu.make_async_copy(x_in.at[m], x_ref.at[m], x_sem.at[m])

    def w_copy(n):
        src, dst = ((w1_in, w1_ref), (w2_in, w2_ref), (w3_in, w3_ref))[n]
        return pltpu.make_async_copy(src, dst, w_sem.at[n])

    def cot_copy(m):
        return pltpu.make_async_copy(cot_ref.at[m], up.at[m], cot_sem.at[m])

    def gin_copy(m):
        return pltpu.make_async_copy(gin_ref.at[m], gin_out.at[m], gin_sem.at[m])

    w_copy(0).start()
    x_copy(0).start()
    w_copy(1).start()
    w_copy(2).start()
    for m in range(1, micros):
        x_copy(m).start()

    barrier = pltpu.get_barrier_semaphore()

    def greet(cond, target):
        @pl.when(cond)
        def _():
            pl.semaphore_signal(barrier, inc=1, device_id=target, device_id_type=pl.DeviceIdType.MESH)

    greet(has_above, {"tile": tile - 1})
    greet(has_below, {"tile": tile + 1})
    greet(chip_above, {"tile": tile - 2})
    greet(chip_below, {"tile": tile + 2})
    greet(sec > 0, {"section": sec - 1})
    greet(sec < sections - 1, {"section": sec + 1})

    @pl.when(is_last)
    def _():
        for m in range(micros):
            cot_copy(m).start()

    def clear_rim(pad):
        tall, wide = pad.shape[1], pad.shape[2]
        for m in range(micros):
            for y in (0, tall - 1):
                pad[m, y] = jnp.zeros((wide, bottle), F32)
            for y in range(1, tall - 1):
                for c in (0, wide - PAD):
                    pad[m, y, pl.ds(c, PAD)] = jnp.zeros((PAD, bottle), F32)

    clear_rim(act_pad)

    def remote(src, dst, ss, rs, target):
        return pltpu.make_async_remote_copy(
            src_ref=src, dst_ref=dst, send_sem=ss, recv_sem=rs,
            device_id=target, device_id_type=pl.DeviceIdType.MESH,
        )

    def fe_up(m):
        return remote(fe_out.at[m, 0], fe_in.at[m, 1], fe_ss.at[m, 0], fe_rs.at[m, 1], {"tile": tile - 1})

    def fe_down(m):
        return remote(fe_out.at[m, 1], fe_in.at[m, 0], fe_ss.at[m, 1], fe_rs.at[m, 0], {"tile": tile + 1})

    def cut(j):
        return pl.ds(*cuts[j])

    def be_up(m, j):
        n = m * pieces + j
        return remote(
            be_out.at[m, 0, cut(j)], be_in.at[m, 1, cut(j)], be_ss.at[n, 0], be_rs.at[n, 1],
            {"tile": tile - 1},
        )

    def be_down(m, j):
        n = m * pieces + j
        return remote(
            be_out.at[m, 1, cut(j)], be_in.at[m, 0, cut(j)], be_ss.at[n, 1], be_rs.at[n, 0],
            {"tile": tile + 1},
        )

    def relay(m, j):
        n = m * pieces + j
        return remote(
            gin_ref.at[m, :, cut(j)], up.at[m, :, cut(j)], up_ss.at[n], up_rs.at[n],
            {"section": sec - 1},
        )

    def reduce_in(m, _):
        x_copy(m).wait()
        for y in range(rows):
            pre = dot_nn(x_ref[m, y], w1_ref[...]) + b1_ref[...]
            act, slope = silu_and_slope(pre)
            slope1[m, y] = slope
            act = act.astype(BF)
            act_pad[m, y + 1, pl.ds(PAD, cols)] = act.astype(F32)
            if y == 0:
                fe_out[m, 0] = act
            if y == rows - 1:
                fe_out[m, 1] = act
        return 0

    w_copy(0).wait()
    reduce_in(0, 0)

    greetings = (
        has_above.astype(jnp.int32) + has_below.astype(jnp.int32) + chip_above.astype(jnp.int32)
        + chip_below.astype(jnp.int32) + (sec > 0).astype(jnp.int32) + (sec < sections - 1).astype(jnp.int32)
    )
    pl.semaphore_wait(barrier, greetings)

    def share_rims(m):
        @pl.when(has_above)
        def _():
            fe_up(m).start()

        @pl.when(has_below)
        def _():
            fe_down(m).start()

    def reduce_and_share(m, _):
        reduce_in(m, 0)
        share_rims(m)
        return 0

    share_rims(0)
    w_copy(1).wait()
    w_copy(2).wait()
    for n in range(model // bottle):
        lanes = pl.ds(n * bottle, bottle)
        t1[:, lanes] = w1_ref[lanes, :].astype(F32).T.astype(BF)
        t3[lanes, :] = w3_ref[:, lanes].astype(F32).T.astype(BF)
    for n in range(9):
        band = pl.ds(n * bottle, bottle)
        t2[band, :] = w2_ref[band, :].astype(F32).T.astype(BF)
    clear_rim(g_pad)
    sum1[...] = jnp.zeros(sum1.shape, F32)
    sum2[...] = jnp.zeros(sum2.shape, F32)
    sum3[...] = jnp.zeros(sum3.shape, F32)

    def expand_out(m, _):
        @pl.when(has_above)
        def _():
            fe_down(m).wait_recv()
            act_pad[m, 0, pl.ds(PAD, cols)] = fe_in[m, 0].astype(F32)

        @pl.when(has_below)
        def _():
            fe_up(m).wait_recv()
            act_pad[m, rows + 1, pl.ds(PAD, cols)] = fe_in[m, 1].astype(F32)

        for shift in range(3):
            for y in range(rows + 2):
                taps[shift, m, y] = act_pad[m, y, pl.ds(PAD - 1 + shift, cols)].astype(BF)
        for y in range(rows):
            patch = jnp.concatenate(
                [taps[dx, m, y + dy] for dy in range(3) for dx in range(3)], axis=-1
            )
            pre = dot_nn(patch, w2_ref[...]) + b2_ref[...]
            act, slope = silu_and_slope(pre)
            slope2[m, y] = slope
            act = act.astype(BF)
            act2[m, y] = act
            for n in range(model // bottle):
                lanes = pl.ds(n * bottle, bottle)
                pre = dot_nn(act, w3_ref[:, lanes]) + b3_ref[:, lanes] + x_ref[m, y, :, lanes].astype(F32)
                slope3[m, y, :, lanes] = silu_and_slope(pre)[1]
        return 0

    def outer_part(m, first, last):
        turn = lax.rem(m, 2)
        begin = cuts[first][0]
        width = sum(cuts[last]) - begin
        span = pl.ds(begin, width)
        for y in range(rows):
            g3[turn, y, span] = (up[m, y, span].astype(F32) * slope3[m, y, span]).astype(BF)
        back = dot_nn(g3[turn, :, span].reshape(rows * width, model), t3[...])
        grad = (back.reshape(rows, width, bottle) * slope2[m, :, span]).astype(BF)
        g2[turn, :, span] = grad
        g_pad[m, pl.ds(1, rows), pl.ds(PAD + begin, width)] = grad.astype(F32)
        be_out[m, 0, span] = grad[0]
        be_out[m, 1, span] = grad[rows - 1]

        @pl.when(has_above)
        def _():
            for j in range(first, last + 1):
                be_up(m, j).start()

        @pl.when(has_below)
        def _():
            for j in range(first, last + 1):
                be_down(m, j).start()

    def take_rims(m, j):
        @pl.when(has_above)
        def _():
            be_down(m, j).wait_recv()
            g_pad[m, 0, pl.ds(PAD + cuts[j][0], cuts[j][1])] = be_in[m, 0, cut(j)].astype(F32)

        @pl.when(has_below)
        def _():
            be_up(m, j).wait_recv()
            g_pad[m, rows + 1, pl.ds(PAD + cuts[j][0], cuts[j][1])] = be_in[m, 1, cut(j)].astype(F32)

    def inner_part(m, first, last):
        turn = lax.rem(m, 2)
        begin = cuts[first][0]
        width = sum(cuts[last]) - begin
        span = pl.ds(begin, width)
        moved = [
            g_pad[m, :, pl.ds(PAD + 1 + begin - dx, width)].astype(BF) for dx in range(3)
        ]
        patch = jnp.concatenate(
            [
                moved[dx][2 - dy : 2 - dy + rows].reshape(rows * width, bottle)
                for dy in range(3)
                for dx in range(3)
            ],
            axis=-1,
        )
        total = dot_nn(patch, t2[...])
        grad = (total.reshape(rows, width, bottle) * slope1[m, :, span]).astype(BF)
        g1[turn, :, span] = grad
        flat = grad.reshape(rows * width, bottle)
        for n in range(model // bottle):
            lanes = pl.ds(n * bottle, bottle)
            back = dot_nn(flat, t1[:, lanes]).reshape(rows, width, bottle)
            direct = up[m, :, span, lanes].astype(F32) * slope3[m, :, span, lanes]
            gin_ref[m, :, span, lanes] = (back + direct).astype(BF)

        @pl.when(sec > 0)
        def _():
            for j in range(first, last + 1):
                relay(m, j).start()

        if last == pieces - 1:
            gin_copy(m).start()

    def add_three(m, n):
        lanes = pl.ds(n * bottle, bottle)
        turn = lax.rem(m, 2)
        sum3[:, lanes] += dot_tn(
            act2[m].reshape(pixels, bottle), g3[turn, :, :, lanes].reshape(pixels, bottle)
        )

    def add_two(m, n):
        turn = lax.rem(m, 2)
        patch = taps[n % 3, m, pl.ds(n // 3, rows)].reshape(pixels, bottle)
        sum2[pl.ds(n * bottle, bottle)] += dot_tn(patch, g2[turn].reshape(pixels, bottle))

    def add_one(m, n):
        lanes = pl.ds(n * bottle, bottle)
        turn = lax.rem(m, 2)
        sum1[lanes] += dot_tn(
            x_ref[m, :, :, lanes].reshape(pixels, bottle), g1[turn].reshape(pixels, bottle)
        )

    count = model // bottle
    threes = [functools.partial(add_three, n=n) for n in range(count)]
    twos = [functools.partial(add_two, n=n) for n in range(9)]
    ones = [functools.partial(add_one, n=n) for n in range(count)]
    adds = threes + twos + ones
    final = micros - 1

    @pl.when(is_last)
    def _():
        def stream(m, _):
            expand_out(m, 0)
            cot_copy(m).wait()
            early = min(2, pieces - 1)
            outer_part(m, 0, early)
            if early < pieces - 1:
                outer_part(m, early + 1, pieces - 1)
            taken = 0
            for first in range(0, pieces - 1, 2):
                last = first + 1 if first + 3 < pieces else pieces - 1
                if first > 0 and last < first:
                    continue
                until = min(last + 2, pieces)
                for j in range(taken, until):
                    take_rims(m, j)
                taken = until
                inner_part(m, first, last)
                if last == pieces - 1:
                    break

            @pl.when(m == 0)
            def _():
                lax.fori_loop(1, micros, reduce_and_share, 0)

            @pl.when(m < final)
            def _():
                for add in adds:
                    add(m)

            return 0

        lax.fori_loop(0, micros, stream, 0)

    @pl.when(jnp.logical_not(is_last))
    def _():
        lax.fori_loop(1, micros, reduce_and_share, 0)
        lax.fori_loop(0, micros, expand_out, 0)

        def stream(m, _):
            left = list(adds)
            for j in range(pieces):
                relay(m, j).wait_recv()
                outer_part(m, j, j)
                if j == 0:
                    @pl.when(m > 0)
                    def _():
                        take_rims(m - 1, pieces - 1)
                        inner_part(m - 1, pieces - 2, pieces - 1)

                    continue

                take_rims(m, j - 1)
                if 0 <= j - 2 < pieces - 2:
                    inner_part(m, j - 2, j - 2)
                share = -(-len(left) // (pieces - j))

                @pl.when(m > 0)
                def _():
                    for add in left[:share]:
                        add(m - 1)

                left = left[share:]
            return 0

        lax.fori_loop(0, micros, stream, 0)

    kinds = (
        (sum3, p3, q3, r3, u3, d3, o3_ref),
        (sum2, p2, q2, r2, u2, d2, o2_ref),
        (sum1, p1, q1, r1, u1, d1, o1_ref),
    )

    def swap(kind):
        return remote(kinds[kind][1], kinds[kind][2], a_ss.at[kind], a_rs.at[kind], {"tile": partner})

    def hop_down(kind, d):
        n = kind * half + d
        return remote(
            kinds[kind][3].at[d], kinds[kind][4].at[d], z_ss.at[n], zd_rs.at[n], {"tile": tile + 2}
        )

    def hop_up(kind, d):
        n = kind * half + d
        return remote(
            kinds[kind][3].at[d], kinds[kind][5].at[d], z_ss.at[n], zu_rs.at[n], {"tile": tile - 2}
        )

    def start_swap(kind):
        total, sent, out = kinds[kind][0], kinds[kind][1], kinds[kind][6]
        span = out.shape[0]
        for z in range(half):
            first = pl.multiple_of((2 * z + 1 - core) * span, 16)
            sent[z] = total[pl.ds(first, span)].astype(BF)
        swap(kind).start()

    def make_part(kind):
        total, _, got, part, _, _, out = kinds[kind]
        span = out.shape[0]
        swap(kind).wait_recv()
        for z in range(half):
            first = pl.multiple_of((2 * z + core) * span, 16)
            part[z] = (total[pl.ds(first, span)] + got[z].astype(F32)).astype(BF)
        own = pl.multiple_of((2 * zed + core) * span, 16)
        out[...] = total[pl.ds(own, span)] + got[zed].astype(F32)

    def send_ends(kind, step):
        @pl.when(jnp.logical_not(chip_above))
        def _():
            hop_down(kind, half - 1 - step).start()

        @pl.when(jnp.logical_not(chip_below))
        def _():
            hop_up(kind, step).start()

    def carry_down(kind, step):
        part, down = kinds[kind][3], kinds[kind][4]
        d = half - 1 - step

        @pl.when(jnp.logical_and(chip_above, zed < d))
        def _():
            hop_down(kind, d).wait_recv()
            part[d] = (part[d].astype(F32) + down[d].astype(F32)).astype(BF)
            hop_down(kind, d).start()

    def carry_up(kind, step):
        part, over = kinds[kind][3], kinds[kind][5]

        @pl.when(jnp.logical_and(chip_below, zed > step))
        def _():
            hop_up(kind, step).wait_recv()
            part[step] = (part[step].astype(F32) + over[step].astype(F32)).astype(BF)
            hop_up(kind, step).start()

    def end_chain(kind):
        _, _, _, _, down, over, out = kinds[kind]

        @pl.when(chip_above)
        def _():
            hop_down(kind, zed).wait_recv()
            out[...] += down[zed].astype(F32)

        @pl.when(chip_below)
        def _():
            hop_up(kind, zed).wait_recv()
            out[...] += over[zed].astype(F32)

    for add in twos:
        add(final)
    start_swap(1)
    for add in threes:
        add(final)
    start_swap(0)
    make_part(1)
    send_ends(1, 0)

    @pl.when(jnp.logical_not(is_last))
    def _():
        take_rims(final, pieces - 1)
        inner_part(final, pieces - 2, pieces - 1)

    for add in ones:
        add(final)
    start_swap(2)
    make_part(0)
    send_ends(0, 0)
    make_part(2)
    send_ends(2, 0)
    order = (1, 0, 2)
    for step in range(1, half - 1):
        for kind in order:
            send_ends(kind, step)
    upper = zed < half // 2
    for near, carries in ((upper, (carry_down, carry_up)), (jnp.logical_not(upper), (carry_up, carry_down))):
        @pl.when(near)
        def _():
            for step in range(half - 1):
                for carry in carries:
                    for kind in order:
                        carry(kind, step)


    def close(m, _):
        gin_copy(m).wait()

        @pl.when(has_above)
        def _():
            fe_up(m).wait_send()
            for j in range(pieces):
                be_up(m, j).wait_send()

        @pl.when(has_below)
        def _():
            fe_down(m).wait_send()
            for j in range(pieces):
                be_down(m, j).wait_send()

        @pl.when(sec > 0)
        def _():
            for j in range(pieces):
                relay(m, j).wait_send()

        return 0

    lax.fori_loop(0, micros, close, 0)
    for kind in range(3):
        end_chain(kind)
    for kind in range(3):
        swap(kind).wait_send()
        for d in range(half):
            @pl.when(zed < d)
            def _():
                hop_down(kind, d).wait_send()

            @pl.when(zed > d)
            def _():
                hop_up(kind, d).wait_send()


def cut_columns(cols):
    wide = (cols - 2 * TAPER) // WIDTH
    cuts = [(n * WIDTH, WIDTH) for n in range(wide)]
    return cuts + [(n, TAPER) for n in range(wide * WIDTH, cols, TAPER)]


def hand_over(*refs):
    count = len(refs) // 4
    ins, outs, holds, sems = (refs[n * count : (n + 1) * count] for n in range(4))
    arrive, leave = [], []
    for a, o, h, s in zip(ins, outs, holds, sems):
        for n in range(h.shape[0] if len(h.shape) > 2 else 1):
            pick = (lambda r: r.at[n]) if len(h.shape) > 2 else (lambda r: r)
            arrive.append(pltpu.make_async_copy(pick(a), pick(h), s.at[0, n]))
            leave.append(pltpu.make_async_copy(pick(h), pick(o), s.at[1, n]))
    for copy in arrive:
        copy.start()
    for one, two in zip(arrive, leave):
        one.wait()
        two.start()
    for copy in leave:
        copy.wait()


def local(
    sections, tiles,
    stored_inputs, cotangent, w_reduce, w_spatial, w_expand, bias_reduce, bias_spatial, bias_expand,
):
    _, micros, rows, cols, model = stored_inputs.shape
    bottle = w_reduce.shape[2]
    half = tiles // 2
    spans = (model // tiles, 9 * bottle // tiles, bottle // tiles)
    wides = (bottle, bottle, model)
    vmem = pltpu.VMEM
    dma = pltpu.SemaphoreType.DMA
    whole = pl.BlockSpec(memory_space=pltpu.VMEM)
    there = pl.BlockSpec(memory_space=pl.ANY)
    scratch = [
        vmem((micros, rows, cols, model), BF),
        vmem((model, bottle), BF),
        vmem((9 * bottle, bottle), BF),
        vmem((bottle, model), BF),
        vmem((micros, rows, cols, model), BF),
        vmem((micros, rows, cols, model), BF),
        vmem((micros, rows, cols, bottle), F32),
        vmem((micros, rows, cols, bottle), F32),
        vmem((micros, rows, cols, model), F32),
        vmem((micros, rows + 2, cols + 2 * PAD, bottle), F32),
        vmem((3, micros, rows + 2, cols, bottle), BF),
        vmem((micros, rows, cols, bottle), BF),
        vmem((micros, rows + 2, cols + 2 * PAD, bottle), F32),
        vmem((2, rows, cols, model), BF),
        vmem((2, rows, cols, bottle), BF),
        vmem((2, rows, cols, bottle), BF),
    ]
    scratch += [vmem((bottle, model), BF), vmem((9 * bottle, bottle), BF), vmem((model, bottle), BF)]
    scratch += [vmem((micros, 2, cols, bottle), BF)] * 4
    scratch += [vmem((span * tiles, wide), F32) for span, wide in zip(spans, wides)]
    for _ in range(5):
        scratch += [vmem((half, span, wide), BF) for span, wide in zip(spans, wides)]
    pieces = micros * len(cut_columns(cols))
    scratch += [
        dma((micros,)), dma((3,)), dma((micros,)),
        dma((micros,)), dma((pieces,)), dma((pieces,)), dma((micros, 2)), dma((micros, 2)),
        dma((pieces, 2)), dma((pieces, 2)), dma((3,)), dma((3,)), dma((3 * half,)), dma((3 * half,)), dma((3 * half,)),
    ]
    shapes = [jax.ShapeDtypeStruct((micros, rows, cols, model), BF)] + [
        jax.ShapeDtypeStruct((span, wide), F32) for span, wide in zip(spans, wides)
    ]
    outs = pl.pallas_call(
        functools.partial(kernel, sections, tiles),
        out_shape=shapes,
        in_specs=[there] * 5 + [whole] * 3,
        out_specs=[there] + [whole] * 3,
        scratch_shapes=scratch,
        compiler_params=pltpu.CompilerParams(
            collective_id=0, has_side_effects=True, vmem_limit_bytes=66 * 1024 * 1000
        ),
    )(
        stored_inputs[0], cotangent, w_reduce[0], w_spatial[0], w_expand[0],
        bias_reduce, bias_spatial, bias_expand,
    )
    outs = pl.pallas_call(
        hand_over,
        out_shape=shapes,
        in_specs=[there] * 4,
        out_specs=[there] * 4,
        scratch_shapes=[vmem(shape.shape, shape.dtype) for shape in shapes] + [dma((2, micros))] * 4,
    )(*outs)
    return tuple(out[None] for out in outs)


def solution(mesh):
    return jax.shard_map(
        functools.partial(local, mesh.shape["section"], mesh.shape["tile"]),
        mesh=mesh,
        in_specs=(
            P("section", None, "tile", None, None),
            P(None, "tile", None, None),
            P("section", None, None),
            P("section", None, None),
            P("section", None, None),
            P("section", None),
            P("section", None),
            P("section", None),
        ),
        out_specs=(
            P("section", None, "tile", None, None),
            P("section", "tile", None),
            P("section", "tile", None),
            P("section", "tile", None),
        ),
        check_vma=False,
    )
```

time: 150 us -> 136 us (0.907)
  Pallas kernels: 143 us -> 135 us
  local copies, waits for them, and re-layouts: 5.95 us -> 0 us
    pallas_call x1 -> x2, Pallas kernels: 143 us -> 135 us  [the longest x1 132 us: local(): pl.pallas_call(functools.partial(kernel, sections, tiles), out_shape=shap...]
    unnamed x10 -> x0, local copies, waits for them, and re-layouts: 5.95 us -> none
where the time goes in v1:
time: 136 us
  Pallas kernels  135 us (99%)
    pallas_call x1, Pallas kernels, local(): pl.pallas_call(functools.partial(kernel, sections, tiles), out_shape=shap...  132 us
    pallas_call x1, Pallas kernels, local(): pl.pallas_call(hand_over, out_shape=shapes, in_specs=[there] * 4, out_spe...  3.25 us

profile of v1, /device:TPU:0, one launch (start us, length us, event | category | flops | bytes accessed | tf_op | source)
XLA Modules:
  0.0 135.6 jit_solution(15896652253140204691)
XLA Ops:
  0.6 131.6 %shard_map.111 = (bf16[4,3,128,1024]{3,2,1,0:T(8,128)(2,1)}, f32[128,256]{1,0:T(8,128)}, f32[288,256]{1,0:T(8,128)}, f32[32,1024]{1,0:T(8,128)}) custom-call(bf16[4,3,128,1024]{3,2,1,0:T(8,128)(2,1)} %bitcast.8, bf16[4,3,128,1024]{3,2,1,0:T(8,128)(2,1)} %cot_ref.1, bf16[1024,256]{1,0:T(8,128)(2,1)} %bitcast.10, bf16[2304,256]{1,0:T(8,128)(2,1)} %bitcast.9, ...), custom_call_target="tpu_custom_call" | custom-call | tf_op jit(solution)/shard_map/pallas_call | solution.py:607
  132.2 3.2 %shard_map.112 = (bf16[4,3,128,1024]{3,2,1,0:T(8,128)(2,1)}, f32[128,256]{1,0:T(8,128)}, f32[288,256]{1,0:T(8,128)}, f32[32,1024]{1,0:T(8,128)}) custom-call(bf16[4,3,128,1024]{3,2,1,0:T(8,128)(2,1)} %get-tuple-element.12.refs_0_, f32[128,256]{1,0:T(8,128)} %get-tuple-element.13.refs_1_, f32[288,256]{1,0:T(8,128)} %get-tuple-element.14.refs_2_, ...), custom_call_target="tpu_custom_call" | custom-call | tf_op jit(solution)/shard_map/pallas_call | solution.py:620

commit v2 on v1

--- a/solution.py
+++ b/solution.py
@@ -10,8 +10,9 @@
 BF = jnp.bfloat16
 F32 = jnp.float32
 PAD = 8
-WIDTH = 16
-TAPER = 8
+WIDTH = 8
+LAG = 3
+GROUP = 4
 
 
 def silu_and_slope(pre_act):
@@ -141,16 +142,13 @@
 
     def reduce_in(m, _):
         x_copy(m).wait()
-        for y in range(rows):
-            pre = dot_nn(x_ref[m, y], w1_ref[...]) + b1_ref[...]
-            act, slope = silu_and_slope(pre)
-            slope1[m, y] = slope
-            act = act.astype(BF)
-            act_pad[m, y + 1, pl.ds(PAD, cols)] = act.astype(F32)
-            if y == 0:
-                fe_out[m, 0] = act
-            if y == rows - 1:
-                fe_out[m, 1] = act
+        pre = dot_nn(x_ref[m].reshape(pixels, model), w1_ref[...]) + b1_ref[...]
+        act, slope = silu_and_slope(pre)
+        slope1[m] = slope.reshape(rows, cols, bottle)
+        act = act.astype(BF).reshape(rows, cols, bottle)
+        act_pad[m, pl.ds(1, rows), pl.ds(PAD, cols)] = act.astype(F32)
+        fe_out[m, 0] = act[0]
+        fe_out[m, 1] = act[rows - 1]
         return 0
 
     w_copy(0).wait()
@@ -187,11 +185,8 @@
         band = pl.ds(n * bottle, bottle)
         t2[band, :] = w2_ref[band, :].astype(F32).T.astype(BF)
     clear_rim(g_pad)
-    sum1[...] = jnp.zeros(sum1.shape, F32)
-    sum2[...] = jnp.zeros(sum2.shape, F32)
-    sum3[...] = jnp.zeros(sum3.shape, F32)
-
-    def expand_out(m, _):
+
+    def take_edges(m):
         @pl.when(has_above)
         def _():
             fe_down(m).wait_recv()
@@ -202,38 +197,50 @@
             fe_up(m).wait_recv()
             act_pad[m, rows + 1, pl.ds(PAD, cols)] = fe_in[m, 1].astype(F32)
 
+    def expand_part(m, begin, width):
+        span = pl.ds(begin, width)
+        area = rows * width
         for shift in range(3):
             for y in range(rows + 2):
-                taps[shift, m, y] = act_pad[m, y, pl.ds(PAD - 1 + shift, cols)].astype(BF)
-        for y in range(rows):
-            patch = jnp.concatenate(
-                [taps[dx, m, y + dy] for dy in range(3) for dx in range(3)], axis=-1
-            )
-            pre = dot_nn(patch, w2_ref[...]) + b2_ref[...]
-            act, slope = silu_and_slope(pre)
-            slope2[m, y] = slope
-            act = act.astype(BF)
-            act2[m, y] = act
-            for n in range(model // bottle):
-                lanes = pl.ds(n * bottle, bottle)
-                pre = dot_nn(act, w3_ref[:, lanes]) + b3_ref[:, lanes] + x_ref[m, y, :, lanes].astype(F32)
-                slope3[m, y, :, lanes] = silu_and_slope(pre)[1]
+                taps[shift, m, y, span] = act_pad[m, y, pl.ds(PAD - 1 + shift + begin, width)].astype(BF)
+        patch = jnp.concatenate(
+            [
+                taps[dx, m, pl.ds(dy, rows), span].reshape(area, bottle)
+                for dy in range(3)
+                for dx in range(3)
+            ],
+            axis=-1,
+        )
+        pre = dot_nn(patch, w2_ref[...]) + b2_ref[...]
+        act, slope = silu_and_slope(pre)
+        slope2[m, :, span] = slope.reshape(rows, width, bottle)
+        act = act.astype(BF)
+        act2[m, :, span] = act.reshape(rows, width, bottle)
+        for n in range(model // bottle):
+            lanes = pl.ds(n * bottle, bottle)
+            pre = dot_nn(act, w3_ref[:, lanes]) + b3_ref[:, lanes]
+            pre = pre + x_ref[m, :, span, lanes].reshape(area, bottle).astype(F32)
+            slope3[m, :, span, lanes] = silu_and_slope(pre)[1].reshape(rows, width, bottle)
+
+    def expand_out(m, _):
+        take_edges(m)
+        expand_part(m, 0, cols)
         return 0
 
     def outer_part(m, first, last):
-        turn = lax.rem(m, 2)
         begin = cuts[first][0]
         width = sum(cuts[last]) - begin
         span = pl.ds(begin, width)
         for y in range(rows):
-            g3[turn, y, span] = (up[m, y, span].astype(F32) * slope3[m, y, span]).astype(BF)
-        back = dot_nn(g3[turn, :, span].reshape(rows * width, model), t3[...])
+            g3[m, y, span] = (up[m, y, span].astype(F32) * slope3[m, y, span]).astype(BF)
+        back = dot_nn(g3[m, :, span].reshape(rows * width, model), t3[...])
         grad = (back.reshape(rows, width, bottle) * slope2[m, :, span]).astype(BF)
-        g2[turn, :, span] = grad
+        g2[m, :, span] = grad
         g_pad[m, pl.ds(1, rows), pl.ds(PAD + begin, width)] = grad.astype(F32)
         be_out[m, 0, span] = grad[0]
         be_out[m, 1, span] = grad[rows - 1]
 
+    def send_rims(m, first, last):
         @pl.when(has_above)
         def _():
             for j in range(first, last + 1):
@@ -256,7 +263,6 @@
             g_pad[m, rows + 1, pl.ds(PAD + cuts[j][0], cuts[j][1])] = be_in[m, 1, cut(j)].astype(F32)
 
     def inner_part(m, first, last):
-        turn = lax.rem(m, 2)
         begin = cuts[first][0]
         width = sum(cuts[last]) - begin
         span = pl.ds(begin, width)
@@ -273,7 +279,7 @@
         )
         total = dot_nn(patch, t2[...])
         grad = (total.reshape(rows, width, bottle) * slope1[m, :, span]).astype(BF)
-        g1[turn, :, span] = grad
+        g1[m, :, span] = grad
         flat = grad.reshape(rows * width, bottle)
         for n in range(model // bottle):
             lanes = pl.ds(n * bottle, bottle)
@@ -281,6 +287,7 @@
             direct = up[m, :, span, lanes].astype(F32) * slope3[m, :, span, lanes]
             gin_ref[m, :, span, lanes] = (back + direct).astype(BF)
 
+    def send_grads(m, first, last):
         @pl.when(sec > 0)
         def _():
             for j in range(first, last + 1):
@@ -289,99 +296,34 @@
         if last == pieces - 1:
             gin_copy(m).start()
 
-    def add_three(m, n):
+    def add_up(total, where, left, right, first, last):
+        deep = (last - first) * pixels
+        value = dot_tn(left.reshape(deep, bottle), right.reshape(deep, bottle))
+        if first > 0:
+            value = value + total[where]
+        total[where] = value
+
+    def add_three(n, first, last):
         lanes = pl.ds(n * bottle, bottle)
-        turn = lax.rem(m, 2)
-        sum3[:, lanes] += dot_tn(
-            act2[m].reshape(pixels, bottle), g3[turn, :, :, lanes].reshape(pixels, bottle)
-        )
-
-    def add_two(m, n):
-        turn = lax.rem(m, 2)
-        patch = taps[n % 3, m, pl.ds(n // 3, rows)].reshape(pixels, bottle)
-        sum2[pl.ds(n * bottle, bottle)] += dot_tn(patch, g2[turn].reshape(pixels, bottle))
-
-    def add_one(m, n):
+        ms = pl.ds(first, last - first)
+        add_up(sum3, (slice(None), lanes), act2[ms], g3[ms, :, :, lanes], first, last)
+
+    def add_two(n, first, last):
+        ms = pl.ds(first, last - first)
+        patch = taps[n % 3, ms, pl.ds(n // 3, rows)]
+        add_up(sum2, (pl.ds(n * bottle, bottle), slice(None)), patch, g2[ms], first, last)
+
+    def add_one(n, first, last):
         lanes = pl.ds(n * bottle, bottle)
-        turn = lax.rem(m, 2)
-        sum1[lanes] += dot_tn(
-            x_ref[m, :, :, lanes].reshape(pixels, bottle), g1[turn].reshape(pixels, bottle)
-        )
+        ms = pl.ds(first, last - first)
+        add_up(sum1, (lanes, slice(None)), x_ref[ms, :, :, lanes], g1[ms], first, last)
 
     count = model // bottle
-    threes = [functools.partial(add_three, n=n) for n in range(count)]
-    twos = [functools.partial(add_two, n=n) for n in range(9)]
-    ones = [functools.partial(add_one, n=n) for n in range(count)]
+    threes = [functools.partial(add_three, n) for n in range(count)]
+    twos = [functools.partial(add_two, n) for n in range(9)]
+    ones = [functools.partial(add_one, n) for n in range(count)]
     adds = threes + twos + ones
     final = micros - 1
-
-    @pl.when(is_last)
-    def _():
-        def stream(m, _):
-            expand_out(m, 0)
-            cot_copy(m).wait()
-            early = min(2, pieces - 1)
-            outer_part(m, 0, early)
-            if early < pieces - 1:
-                outer_part(m, early + 1, pieces - 1)
-            taken = 0
-            for first in range(0, pieces - 1, 2):
-                last = first + 1 if first + 3 < pieces else pieces - 1
-                if first > 0 and last < first:
-                    continue
-                until = min(last + 2, pieces)
-                for j in range(taken, until):
-                    take_rims(m, j)
-                taken = until
-                inner_part(m, first, last)
-                if last == pieces - 1:
-                    break
-
-            @pl.when(m == 0)
-            def _():
-                lax.fori_loop(1, micros, reduce_and_share, 0)
-
-            @pl.when(m < final)
-            def _():
-                for add in adds:
-                    add(m)
-
-            return 0
-
-        lax.fori_loop(0, micros, stream, 0)
-
-    @pl.when(jnp.logical_not(is_last))
-    def _():
-        lax.fori_loop(1, micros, reduce_and_share, 0)
-        lax.fori_loop(0, micros, expand_out, 0)
-
-        def stream(m, _):
-            left = list(adds)
-            for j in range(pieces):
-                relay(m, j).wait_recv()
-                outer_part(m, j, j)
-                if j == 0:
-                    @pl.when(m > 0)
-                    def _():
-                        take_rims(m - 1, pieces - 1)
-                        inner_part(m - 1, pieces - 2, pieces - 1)
-
-                    continue
-
-                take_rims(m, j - 1)
-                if 0 <= j - 2 < pieces - 2:
-                    inner_part(m, j - 2, j - 2)
-                share = -(-len(left) // (pieces - j))
-
-                @pl.when(m > 0)
-                def _():
-                    for add in left[:share]:
-                        add(m - 1)
-
-                left = left[share:]
-            return 0
-
-        lax.fori_loop(0, micros, stream, 0)
 
     kinds = (
         (sum3, p3, q3, r3, u3, d3, o3_ref),
@@ -463,25 +405,129 @@
             hop_up(kind, zed).wait_recv()
             out[...] += over[zed].astype(F32)
 
-    for add in twos:
-        add(final)
-    start_swap(1)
-    for add in threes:
-        add(final)
-    start_swap(0)
+    def lead(first):
+        for add in twos:
+            add(first, micros)
+        start_swap(1)
+        for add in threes:
+            add(first, micros)
+        start_swap(0)
+
+    def trail(first):
+        for add in ones:
+            add(first, micros)
+        start_swap(2)
+
+    @pl.when(is_last)
+    def _():
+        def stream(m, _):
+            take_edges(m)
+            cot_copy(m).wait()
+            early = min(GROUP, pieces - 1)
+            for first, last in ((0, early), (early + 1, pieces - 1)):
+                if first <= last:
+                    begin = cuts[first][0]
+                    expand_part(m, begin, sum(cuts[last]) - begin)
+                    outer_part(m, first, last)
+                    send_rims(m, first, last)
+            taken = 0
+            for first in range(0, pieces, GROUP):
+                last = min(first + GROUP, pieces) - 1
+                until = min(last + 2, pieces)
+                for j in range(taken, until):
+                    take_rims(m, j)
+                taken = until
+                inner_part(m, first, last)
+                send_grads(m, first, last)
+
+            @pl.when(m == 0)
+            def _():
+                lax.fori_loop(1, micros, reduce_and_share, 0)
+
+            return 0
+
+        lax.fori_loop(0, micros, stream, 0)
+
+    @pl.when(jnp.logical_not(is_last))
+    def _():
+        lax.fori_loop(1, micros, reduce_and_share, 0)
+        lax.fori_loop(0, micros, expand_out, 0)
+
+        def stream(m, _):
+            left = list(adds)
+            for j in range(pieces):
+                relay(m, j).wait_recv()
+                k = j - LAG - 1
+                if j >= LAG:
+                    take_rims(m, j - LAG)
+                if k >= 0:
+                    outer_part(m, j, j)
+                    inner_part(m, k, k)
+                    send_rims(m, j, j)
+                    send_grads(m, k, k)
+                else:
+                    @pl.when(m == 0)
+                    def _():
+                        outer_part(m, j, j)
+
+                    @pl.when(m > 0)
+                    def _():
+                        if j < LAG:
+                            take_rims(m - 1, pieces + j - LAG)
+                        outer_part(m, j, j)
+                        inner_part(m - 1, pieces + k, pieces + k)
+
+                    send_rims(m, j, j)
+
+                    @pl.when(m > 0)
+                    def _():
+                        send_grads(m - 1, pieces + k, pieces + k)
+
+                if k >= 0 and left:
+                    share = -(-len(left) // (pieces - j))
+
+                    @pl.when(jnp.logical_and(m == final, sec == 0))
+                    def _():
+                        for add in left[:share]:
+                            add(0, final)
+
+                    left = left[share:]
+            return 0
+
+        lax.fori_loop(0, micros, stream, 0)
+
+    alone = jnp.logical_and(sec == 0, jnp.logical_not(is_last))
+
+    @pl.when(alone)
+    def _():
+        lead(final)
+
+    @pl.when(alone)
+    def _():
+        for j in range(pieces - LAG, pieces):
+            take_rims(final, j)
+        inner_part(final, pieces - LAG - 1, pieces - 1)
+        send_grads(final, pieces - LAG - 1, pieces - 1)
+        trail(final)
+
+    @pl.when(jnp.logical_and(sec > 0, jnp.logical_not(is_last)))
+    def _():
+        for j in range(pieces - LAG, pieces):
+            take_rims(final, j)
+            last = j if j == pieces - 1 else j - 1
+            inner_part(final, j - 1, last)
+            send_grads(final, j - 1, last)
+
+    @pl.when(jnp.logical_not(alone))
+    def _():
+        lead(0)
+        trail(0)
+
     make_part(1)
     send_ends(1, 0)
-
-    @pl.when(jnp.logical_not(is_last))
-    def _():
-        take_rims(final, pieces - 1)
-        inner_part(final, pieces - 2, pieces - 1)
-
-    for add in ones:
-        add(final)
-    start_swap(2)
     make_part(0)
     send_ends(0, 0)
+
     make_part(2)
     send_ends(2, 0)
     order = (1, 0, 2)
@@ -536,26 +582,16 @@
 
 
 def cut_columns(cols):
-    wide = (cols - 2 * TAPER) // WIDTH
-    cuts = [(n * WIDTH, WIDTH) for n in range(wide)]
-    return cuts + [(n, TAPER) for n in range(wide * WIDTH, cols, TAPER)]
+    return [(n, WIDTH) for n in range(0, cols, WIDTH)]
 
 
 def hand_over(*refs):
-    count = len(refs) // 4
-    ins, outs, holds, sems = (refs[n * count : (n + 1) * count] for n in range(4))
-    arrive, leave = [], []
-    for a, o, h, s in zip(ins, outs, holds, sems):
-        for n in range(h.shape[0] if len(h.shape) > 2 else 1):
-            pick = (lambda r: r.at[n]) if len(h.shape) > 2 else (lambda r: r)
-            arrive.append(pltpu.make_async_copy(pick(a), pick(h), s.at[0, n]))
-            leave.append(pltpu.make_async_copy(pick(h), pick(o), s.at[1, n]))
-    for copy in arrive:
+    count = len(refs) // 3
+    ins, outs, sems = (refs[n * count : (n + 1) * count] for n in range(3))
+    copies = [pltpu.make_async_copy(a, o, s) for a, o, s in zip(ins, outs, sems)]
+    for copy in copies:
         copy.start()
-    for one, two in zip(arrive, leave):
-        one.wait()
-        two.start()
-    for copy in leave:
+    for copy in copies:
         copy.wait()
 
 
@@ -586,9 +622,9 @@
         vmem((3, micros, rows + 2, cols, bottle), BF),
         vmem((micros, rows, cols, bottle), BF),
         vmem((micros, rows + 2, cols + 2 * PAD, bottle), F32),
-        vmem((2, rows, cols, model), BF),
-        vmem((2, rows, cols, bottle), BF),
-        vmem((2, rows, cols, bottle), BF),
+        vmem((micros, rows, cols, model), BF),
+        vmem((micros, rows, cols, bottle), BF),
+        vmem((micros, rows, cols, bottle), BF),
     ]
     scratch += [vmem((bottle, model), BF), vmem((9 * bottle, bottle), BF), vmem((model, bottle), BF)]
     scratch += [vmem((micros, 2, cols, bottle), BF)] * 4
@@ -606,12 +642,12 @@
     ]
     outs = pl.pallas_call(
         functools.partial(kernel, sections, tiles),
-        out_shape=shapes,
+        out_shape=[vmem(shape.shape, shape.dtype) for shape in shapes],
         in_specs=[there] * 5 + [whole] * 3,
         out_specs=[there] + [whole] * 3,
         scratch_shapes=scratch,
         compiler_params=pltpu.CompilerParams(
-            collective_id=0, has_side_effects=True, vmem_limit_bytes=66 * 1024 * 1000
+            collective_id=0, has_side_effects=True, vmem_limit_bytes=58 * 1024 * 1024
         ),
     )(
         stored_inputs[0], cotangent, w_reduce[0], w_spatial[0], w_expand[0],
@@ -622,8 +658,9 @@
         out_shape=shapes,
         in_specs=[there] * 4,
         out_specs=[there] * 4,
-        scratch_shapes=[vmem(shape.shape, shape.dtype) for shape in shapes] + [dma((2, micros))] * 4,
-    )(*outs)
+        scratch_shapes=[dma] * 4,
+        compiler_params=pltpu.CompilerParams(vmem_limit_bytes=2 * 1024 * 1024),
+    )(*[pltpu.with_memory_space_constraint(out, pltpu.VMEM) for out in outs])
     return tuple(out[None] for out in outs)
 
 

time: 136 us -> 131 us (0.963)
  Pallas kernels: 135 us -> 130 us
    pallas_call x1, Pallas kernels: 132 us -> 128 us  [local(): pl.pallas_call(functools.partial(kernel, sections, tiles), out_shape=[vme...]
    pallas_call x1, Pallas kernels: 3.25 us -> 1.87 us  [local(): pl.pallas_call(hand_over, out_shape=shapes, in_specs=[there] * 4, out_spe...]
where the time goes in v2:
time: 131 us
  Pallas kernels  130 us (99%)
    pallas_call x1, Pallas kernels, local(): pl.pallas_call(functools.partial(kernel, sections, tiles), out_shape=[vme...  128 us

profile of v2, /device:TPU:0, one launch (start us, length us, event | category | flops | bytes accessed | tf_op | source)
XLA Modules:
  0.0 130.5 jit_solution(1432160837762860113)
XLA Ops:
  0.6 127.8 %shard_map.111 = (bf16[4,3,128,1024]{3,2,1,0:T(8,128)(2,1)S(1)}, f32[128,256]{1,0:T(8,128)S(1)}, f32[288,256]{1,0:T(8,128)S(1)}, f32[32,1024]{1,0:T(8,128)S(1)}) custom-call(bf16[4,3,128,1024]{3,2,1,0:T(8,128)(2,1)} %bitcast.8, bf16[4,3,128,1024]{3,2,1,0:T(8,128)(2,1)} %cot_ref.1, bf16[1024,256]{1,0:T(8,128)(2,1)} %bitcast.10, bf16[2304,256]{1,0:T(8,128)(2,1)} %bitcast.9, ...), custom_call_target="tpu_custom_call" | custom-call | tf_op jit(solution)/shard_map/pallas_call | solution.py:643
  128.5 1.9 %shard_map.112 = (bf16[4,3,128,1024]{3,2,1,0:T(8,128)(2,1)}, f32[128,256]{1,0:T(8,128)}, f32[288,256]{1,0:T(8,128)}, f32[32,1024]{1,0:T(8,128)}) custom-call(bf16[4,3,128,1024]{3,2,1,0:T(8,128)(2,1)S(1)} %get-tuple-element.12.refs_0_, f32[128,256]{1,0:T(8,128)S(1)} %get-tuple-element.13.refs_1_, f32[288,256]{1,0:T(8,128)S(1)} %get-tuple-element.14.refs_2_, ...), custom_call_target="tpu_custom_call" | custom-call | tf_op jit(solution)/shard_map/pallas_call | solution.py:656

commit v3 on v2

--- a/solution.py
+++ b/solution.py
@@ -12,7 +12,7 @@
 PAD = 8
 WIDTH = 8
 LAG = 3
-GROUP = 4
+GROUP = 2
 
 
 def silu_and_slope(pre_act):
@@ -69,11 +69,6 @@
 
     w_copy(0).start()
     x_copy(0).start()
-    w_copy(1).start()
-    w_copy(2).start()
-    for m in range(1, micros):
-        x_copy(m).start()
-
     barrier = pltpu.get_barrier_semaphore()
 
     def greet(cond, target):
@@ -87,11 +82,6 @@
     greet(chip_below, {"tile": tile + 2})
     greet(sec > 0, {"section": sec - 1})
     greet(sec < sections - 1, {"section": sec + 1})
-
-    @pl.when(is_last)
-    def _():
-        for m in range(micros):
-            cot_copy(m).start()
 
     def clear_rim(pad):
         tall, wide = pad.shape[1], pad.shape[2]
@@ -141,7 +131,6 @@
         )
 
     def reduce_in(m, _):
-        x_copy(m).wait()
         pre = dot_nn(x_ref[m].reshape(pixels, model), w1_ref[...]) + b1_ref[...]
         act, slope = silu_and_slope(pre)
         slope1[m] = slope.reshape(rows, cols, bottle)
@@ -152,6 +141,17 @@
         return 0
 
     w_copy(0).wait()
+    x_copy(0).wait()
+    w_copy(1).start()
+    w_copy(2).start()
+    for m in range(1, micros):
+        x_copy(m).start()
+
+    @pl.when(is_last)
+    def _():
+        for m in range(micros):
+            cot_copy(m).start()
+
     reduce_in(0, 0)
 
     greetings = (
@@ -170,6 +170,7 @@
             fe_down(m).start()
 
     def reduce_and_share(m, _):
+        x_copy(m).wait()
         reduce_in(m, 0)
         share_rims(m)
         return 0
@@ -484,7 +485,7 @@
                         send_grads(m - 1, pieces + k, pieces + k)
 
                 if k >= 0 and left:
-                    share = -(-len(left) // (pieces - j))
+                    share = -(-len(left) // max(1, pieces - GROUP - LAG - j))
 
                     @pl.when(jnp.logical_and(m == final, sec == 0))
                     def _():
@@ -501,6 +502,8 @@
     @pl.when(alone)
     def _():
         lead(final)
+        make_part(1)
+        send_ends(1, 0)
 
     @pl.when(alone)
     def _():
@@ -521,10 +524,10 @@
     @pl.when(jnp.logical_not(alone))
     def _():
         lead(0)
+        make_part(1)
+        send_ends(1, 0)
         trail(0)
 
-    make_part(1)
-    send_ends(1, 0)
     make_part(0)
     send_ends(0, 0)
 
@@ -588,7 +591,12 @@
 def hand_over(*refs):
     count = len(refs) // 3
     ins, outs, sems = (refs[n * count : (n + 1) * count] for n in range(3))
-    copies = [pltpu.make_async_copy(a, o, s) for a, o, s in zip(ins, outs, sems)]
+    copies = [
+        pltpu.make_async_copy(ins[0].at[m, y], outs[0].at[m, y], sems[0].at[m, y])
+        for m in range(ins[0].shape[0])
+        for y in range(ins[0].shape[1])
+    ]
+    copies += [pltpu.make_async_copy(a, o, s) for a, o, s in zip(ins[1:], outs[1:], sems[1:])]
     for copy in copies:
         copy.start()
     for copy in copies:
@@ -658,7 +666,7 @@
         out_shape=shapes,
         in_specs=[there] * 4,
         out_specs=[there] * 4,
-        scratch_shapes=[dma] * 4,
+        scratch_shapes=[dma((micros, rows))] + [dma] * 3,
         compiler_params=pltpu.CompilerParams(vmem_limit_bytes=2 * 1024 * 1024),
     )(*[pltpu.with_memory_space_constraint(out, pltpu.VMEM) for out in outs])
     return tuple(out[None] for out in outs)

time: 131 us -> 130 us (level)
  Pallas kernels: 130 us -> 128 us
    pallas_call x1, Pallas kernels: 128 us -> 126 us  [local(): pl.pallas_call(functools.partial(kernel, sections, tiles), out_shape=[vme...]
where the time goes in v3:
time: 130 us; the launch traced here: 129 us
  Pallas kernels  128 us (98%)
    pallas_call x1, Pallas kernels, local(): pl.pallas_call(functools.partial(kernel, sections, tiles), out_shape=[vme...  126 us

profile of v3, /device:TPU:0, one launch (start us, length us, event | category | flops | bytes accessed | tf_op | source)
XLA Modules:
  0.0 128.6 jit_solution(15737129595520089958)
XLA Ops:
  0.6 125.9 %shard_map.111 = (bf16[4,3,128,1024]{3,2,1,0:T(8,128)(2,1)S(1)}, f32[128,256]{1,0:T(8,128)S(1)}, f32[288,256]{1,0:T(8,128)S(1)}, f32[32,1024]{1,0:T(8,128)S(1)}) custom-call(bf16[4,3,128,1024]{3,2,1,0:T(8,128)(2,1)} %bitcast.8, bf16[4,3,128,1024]{3,2,1,0:T(8,128)(2,1)} %cot_ref.1, bf16[1024,256]{1,0:T(8,128)(2,1)} %bitcast.10, bf16[2304,256]{1,0:T(8,128)(2,1)} %bitcast.9, ...), custom_call_target="tpu_custom_call" | custom-call | tf_op jit(solution)/shard_map/pallas_call | solution.py:651
  126.5 2.0 %shard_map.112 = (bf16[4,3,128,1024]{3,2,1,0:T(8,128)(2,1)}, f32[128,256]{1,0:T(8,128)}, f32[288,256]{1,0:T(8,128)}, f32[32,1024]{1,0:T(8,128)}) custom-call(bf16[4,3,128,1024]{3,2,1,0:T(8,128)(2,1)S(1)} %get-tuple-element.12.refs_0_, f32[128,256]{1,0:T(8,128)S(1)} %get-tuple-element.13.refs_1_, f32[288,256]{1,0:T(8,128)S(1)} %get-tuple-element.14.refs_2_, ...), custom_call_target="tpu_custom_call" | custom-call | tf_op jit(solution)/shard_map/pallas_call | solution.py:664
